TPU v7x, 512 devices: a whole 4x4x16 slice. The times are simulated.
512 devices in a mesh: row: 32 (over x, y, core), pair: 16 (over z).
Axes of the slice: x: 4, y: 4, z: 16, core: 2. Of those that a mesh axis runs over, the one named last changes fastest.
Arguments:
- matrix: float32 [65536, 2048], P('row', 'pair'), may hold values from -80 to 80
- partner: int32 [3, 16], replicated, may hold values from 0 to 15, as said below
Outputs:
- result: float32 [65536, 2048], P('row', 'pair')
Inputs may be any that keep to these rules, and one draw needn't show every extreme that they name: partner[r, j] equals j XOR s_r, where s_r is a power of two below 16 and the same for every j of round r.
All inputs are finite; a program needn't handle non-finite values.
Results may differ from a plain program's by a relative error of at most 0.0003.
Values sent between devices are 32-bit elements; how exact they have to be, the bound alone decides.
A program may use at most 64 MiB of HBM per device.

v0:
```python
import jax
import jax.numpy as jnp
from jax import lax
from jax.sharding import PartitionSpec as P

ROUNDS = 4
NS_ITERS = 6


def partner_2(value, axis, stride):
    mask = 2**stride
    pairs = [(source, source ^ mask) for source in range(lax.axis_size(axis))]
    return lax.ppermute(value, axis, pairs)


def orthogonalizer(gram):
    identity = jnp.eye(gram.shape[0], dtype=jnp.float32)
    frobenius = jnp.sqrt(jnp.sum(gram * gram))
    square_root = gram / frobenius
    inverse_root = identity
    for step_count in range(NS_ITERS):
        correction = 1.5 * identity - 0.5 * jnp.dot(
            inverse_root, square_root, precision=lax.Precision.HIGHEST
        )
        square_root = jnp.dot(square_root, correction, precision=lax.Precision.HIGHEST)
        inverse_root = jnp.dot(correction, inverse_root, precision=lax.Precision.HIGHEST)
    return inverse_root * (jnp.sqrt(jnp.diagonal(gram)) / jnp.sqrt(frobenius))[None, :]


def full_gram(columns):
    local_gram = jnp.dot(columns.T, columns, precision=lax.Precision.HIGHEST)
    return lax.psum(local_gram, "row")


def swap_branch(bit_index):

    def apply_swap(folded):
        return partner_2(folded, "pair", bit_index)

    return apply_swap


def body(matrix, partner):
    rows_here, width = matrix.shape
    half_width = width // 2
    pair_count = lax.axis_size("pair")
    bit_total = pair_count.bit_length() - 1
    my_pair = lax.axis_index("pair")
    columns = matrix
    gram = full_gram(columns)
    for round_index in range(ROUNDS):
        rotation = orthogonalizer(gram)
        columns = jnp.dot(columns, rotation, precision=lax.Precision.HIGHEST)
        if round_index + 1 < ROUNDS:
            offset = jnp.bitwise_xor(partner[round_index, my_pair], my_pair)
            folded = columns[:, half_width:].reshape(rows_here // 2, width)
            positions = jnp.arange(bit_total, dtype=jnp.int32)
            which_bit = jnp.sum(jnp.bitwise_and(jnp.right_shift(offset, positions), 1) * positions)
            folded = lax.switch(
                which_bit, [swap_branch(bit_index) for bit_index in range(bit_total)], folded
            )
            second = folded.reshape(rows_here, half_width)
            first = columns[:, :half_width]
            new_columns = jnp.concatenate([first, second], axis=1)
            columns = new_columns
            gram = full_gram(columns)
    return columns


def solution(mesh):
    in_specs = (P("row", "pair"), P())
    out_specs = P("row", "pair")
    return jax.shard_map(body, mesh=mesh, in_specs=in_specs, out_specs=out_specs, check_vma=False)
```

profile of v0, /device:TPU:1, one launch (start us, length us, event | category | flops | bytes accessed | tf_op | source)
XLA Modules:
  0.0 723.2 jit_solution(446828750043776343)
XLA Ops:
  7.8 2.5 fusion.44
  13.5 129.1 %all-reduce.5.cloned.1.call-done = f32[128,128]{1,0:T(8,128)} async-done(((f32[128,128]{1,0:T(8,128)}), f32[128,128]{1,0:T(8,128)}) %all-reduce.5.cloned.1.call-update) | async-done | bytes 65552 | tf_op jit(solution)/shard_map/psum | solution.py:32
  142.6 1.5 multiply_reduce_fusion.3
  150.9 42.5 %conditional.3 = (f32[2048,64]{0,1:T(8,128)S(1)}) conditional(s32[]{:T(128)} %clamp.9, (f32[2048,128]{0,1:T(8,128)S(1)}) %tuple.57, (f32[2048,128]{0,1:T(8,128)S(1)}) %tuple.57, (f32[2048,128]{0,1:T(8,128)S(1)}) %tuple.57, (f32[2048,128]{0,1:T(8,128)S(1)}) %tuple.57), branch_computations={%region_3.4_spmd, %region_4.5_spmd, %region_5.6_spmd, %region_6.7_... | conditional | bytes 8388656 | solution.py:59
  152.2 1.6 slice.62
  154.0 12.6 %collective-permute-start.3 = (f32[1024,128]{1,0:T(8,128)S(1)}, f32[1024,128]{1,0:T(8,128)}, u32[]{:S(2)}, u32[]{:S(2)}) collective-permute-start(f32[1024,128]{1,0:T(8,128)S(1)} %reshape.100), channel_id=1, source_target_pairs={{0,8},{1,9},{2,10},{3,11},{4,12},{5,13},{6,14},{7,15},{8,0},{9,1},... | collective-permute-start | bytes 1572872 | tf_op jit(solution)/shard_map/cond/branch_3_fun/ppermute | solution.py:13
  166.6 25.2 %collective-permute-done.3 = f32[1024,128]{1,0:T(8,128)} collective-permute-done((f32[1024,128]{1,0:T(8,128)S(1)}, f32[1024,128]{1,0:T(8,128)}, u32[]{:S(2)}, u32[]{:S(2)}) %collective-permute-start.3) | collective-permute-done | bytes 524320 | tf_op jit(solution)/shard_map/cond/branch_3_fun/ppermute | solution.py:13
  193.3 1.6 fusion.29
  197.3 143.4 %all-reduce.7.cloned.1.call-done = f32[128,128]{1,0:T(8,128)} async-done(((f32[128,128]{1,0:T(8,128)}), f32[128,128]{1,0:T(8,128)}) %all-reduce.7.cloned.1.call-update) | async-done | bytes 65552 | tf_op jit(solution)/shard_map/psum | solution.py:32
  348.9 42.5 %conditional.4 = (f32[2048,64]{0,1:T(8,128)S(1)}) conditional(s32[]{:T(128)} %clamp.10, (f32[2048,128]{0,1:T(8,128)S(1)}) %tuple.62, (f32[2048,128]{0,1:T(8,128)S(1)}) %tuple.62, (f32[2048,128]{0,1:T(8,128)S(1)}) %tuple.62, (f32[2048,128]{0,1:T(8,128)S(1)}) %tuple.62), branch_computations={%region_10.11_spmd, %region_11.12_spmd, %region_12.13_spmd, %regio... | conditional | bytes 8388656 | solution.py:59
  350.2 1.6 slice.66
  352.0 12.6 %collective-permute-start.7 = (f32[1024,128]{1,0:T(8,128)S(1)}, f32[1024,128]{1,0:T(8,128)}, u32[]{:S(2)}, u32[]{:S(2)}) collective-permute-start(f32[1024,128]{1,0:T(8,128)S(1)} %reshape.108), channel_id=1, source_target_pairs={{0,8},{1,9},{2,10},{3,11},{4,12},{5,13},{6,14},{7,15},{8,0},{9,1},... | collective-permute-start | bytes 1572872 | tf_op jit(solution)/shard_map/cond/branch_3_fun/ppermute | solution.py:13
  364.6 25.2 %collective-permute-done.7 = f32[1024,128]{1,0:T(8,128)} collective-permute-done((f32[1024,128]{1,0:T(8,128)S(1)}, f32[1024,128]{1,0:T(8,128)}, u32[]{:S(2)}, u32[]{:S(2)}) %collective-permute-start.7) | collective-permute-done | bytes 524320 | tf_op jit(solution)/shard_map/cond/branch_3_fun/ppermute | solution.py:13
  391.4 1.6 fusion.27
  395.3 143.4 %all-reduce.9.cloned.1.call-done = f32[128,128]{1,0:T(8,128)} async-done(((f32[128,128]{1,0:T(8,128)}), f32[128,128]{1,0:T(8,128)}) %all-reduce.9.cloned.1.call-update) | async-done | bytes 65552 | tf_op jit(solution)/shard_map/psum | solution.py:32
  538.7 1.5 multiply_reduce_fusion.1
  547.0 32.3 %conditional.5 = (f32[2048,64]{0,1:T(8,128)S(1)}) conditional(s32[]{:T(128)} %clamp.11, (f32[2048,128]{0,1:T(8,128)S(1)}) %tuple.67, (f32[2048,128]{0,1:T(8,128)S(1)}) %tuple.67, (f32[2048,128]{0,1:T(8,128)S(1)}) %tuple.67, (f32[2048,128]{0,1:T(8,128)S(1)}) %tuple.67), branch_computations={%region_17.18_spmd, %region_18.19_spmd, %region_19.20_spmd, %regio... | conditional | bytes 8388656 | solution.py:59
  548.3 1.6 slice.68
  550.1 4.3 collective-permute-start.9
  554.3 23.1 %collective-permute-done.9 = f32[1024,128]{1,0:T(8,128)} collective-permute-done((f32[1024,128]{1,0:T(8,128)S(1)}, f32[1024,128]{1,0:T(8,128)}, u32[]{:S(2)}, u32[]{:S(2)}) %collective-permute-start.9) | collective-permute-done | bytes 524320 | tf_op jit(solution)/shard_map/cond/branch_1_fun/ppermute | solution.py:13
  579.2 1.6 fusion.25
  580.9 125.9 %all-reduce.11.cloned.1.call-done = f32[128,128]{1,0:T(8,128)} async-done(((f32[128,128]{1,0:T(8,128)}), f32[128,128]{1,0:T(8,128)}) %all-reduce.11.cloned.1.call-update) | async-done | bytes 65552 | tf_op jit(solution)/shard_map/psum | solution.py:32
  706.8 1.5 multiply_reduce_fusion
  713.9 2.8 fusion.24
  (120 shorter events, 38.0 us)
Async XLA Ops:
  6.5 1.2 copy-start
  6.5 136.1 %all-reduce.5.cloned.1.call-start = ((), (), s32[]{:S(2)}) async-start(), calls=%async_computation | async-start | bytes 131072 | tf_op jit(solution)/shard_map/psum | solution.py:32
  10.2 330.4 %all-reduce.7.cloned.1.call-start = ((), (), s32[]{:S(2)}) async-start(), calls=%async_computation.1 | async-start | bytes 131072 | tf_op jit(solution)/shard_map/psum | solution.py:32
  10.3 0.7 copy-start.5
  142.6 2.3 copy-start.1
  154.0 37.8 %collective-permute-start.3 = (f32[1024,128]{1,0:T(8,128)S(1)}, f32[1024,128]{1,0:T(8,128)}, u32[]{:S(2)}, u32[]{:S(2)}) collective-permute-start(f32[1024,128]{1,0:T(8,128)S(1)} %reshape.100), channel_id=1, source_target_pairs={{0,8},{1,9},{2,10},{3,11},{4,12},{5,13},{6,14},{7,15},{8,0},{9,1},... | collective-permute-start | bytes 1572872 | tf_op jit(solution)/shard_map/cond/branch_3_fun/ppermute | solution.py:13
  195.0 343.7 %all-reduce.9.cloned.1.call-start = ((), (), s32[]{:S(2)}) async-start(), calls=%async_computation.2 | async-start | bytes 131072 | tf_op jit(solution)/shard_map/psum | solution.py:32
  340.7 2.3 copy-start.3
  352.0 37.8 %collective-permute-start.7 = (f32[1024,128]{1,0:T(8,128)S(1)}, f32[1024,128]{1,0:T(8,128)}, u32[]{:S(2)}, u32[]{:S(2)}) collective-permute-start(f32[1024,128]{1,0:T(8,128)S(1)} %reshape.108), channel_id=1, source_target_pairs={{0,8},{1,9},{2,10},{3,11},{4,12},{5,13},{6,14},{7,15},{8,0},{9,1},... | collective-permute-start | bytes 1572872 | tf_op jit(solution)/shard_map/cond/branch_3_fun/ppermute | solution.py:13
  393.0 313.8 %all-reduce.11.cloned.1.call-start = ((), (), s32[]{:S(2)}) async-start(), calls=%async_computation.3 | async-start | bytes 131072 | tf_op jit(solution)/shard_map/psum | solution.py:32
  538.7 2.3 copy-start.2
  550.1 27.3 %collective-permute-start.9 = (f32[1024,128]{1,0:T(8,128)S(1)}, f32[1024,128]{1,0:T(8,128)}, u32[]{:S(2)}, u32[]{:S(2)}) collective-permute-start(f32[1024,128]{1,0:T(8,128)S(1)} %reshape.112), channel_id=1, source_target_pairs={{0,2},{1,3},{2,0},{3,1},{4,6},{5,7},{6,4},{7,5},{8,10},{9,11},{10,... | collective-permute-start | bytes 1572872 | tf_op jit(solution)/shard_map/cond/branch_1_fun/ppermute | solution.py:13
  706.8 2.3 copy-start.4
Sparse Core Ops, SparseCore 0:
  10.6 131.9 all-reduce.4
  195.1 145.5 all-reduce.6
  393.1 145.5 all-reduce.8
  581.0 125.7 all-reduce.10
where the time goes:
time: 724 us; the launch traced here: 723 us
  waiting for transfers between devices  615 us (85%)
  starting transfers between devices  30 us (4%)
  matrix products  27 us (4%)
  local copies, waits for them, and re-layouts  21.6 us (3%)
  between operations  20.8 us (3%)
  other arithmetic  8.18 us (1%)
    psum x4, waiting for transfers between devices, full_gram(): return lax.psum(local_gram, 'row')  542 us
    ppermute x3, waiting for transfers between devices, partner_2(): return lax.ppermute(value, axis, pairs)  73.4 us
    ppermute x3, starting transfers between devices, partner_2(): return lax.ppermute(value, axis, pairs)  29.5 us
  transfers between devices with their start and end apart: 7, of which 7 were waited for; matrix products, arithmetic and copies ran while one was open for 0% of the time, Pallas kernels for 0%

commit v1 on v0

v1 whole, which is shorter than its diff:
```python
import functools

import jax
import jax.numpy as jnp
from jax import lax
from jax.experimental import pallas as pl
from jax.experimental.pallas import tpu as pltpu
from jax.sharding import PartitionSpec as P

ROUNDS = 4
NS_ITERS = 6
MESH = pl.DeviceIdType.MESH
HIGHEST = lax.Precision.HIGHEST


def dot(a, b):
    return jnp.dot(a, b, precision=HIGHEST, preferred_element_type=jnp.float32)


def orthogonalizer(gram):
    size = gram.shape[0]
    rows = lax.broadcasted_iota(jnp.int32, (size, size), 0)
    cols = lax.broadcasted_iota(jnp.int32, (size, size), 1)
    identity = jnp.where(rows == cols, 1.0, 0.0).astype(jnp.float32)
    square_sum = jnp.sum(jnp.sum(gram * gram, axis=0, keepdims=True), axis=1, keepdims=True)
    frobenius = jnp.sqrt(square_sum)
    root = gram / frobenius
    inverse = 1.5 * identity - 0.5 * root
    root = dot(root, inverse)
    for step in range(1, NS_ITERS):
        correction = 1.5 * identity - 0.5 * dot(inverse, root)
        if step + 1 < NS_ITERS:
            root = dot(root, correction)
        inverse = dot(correction, inverse)
    diagonal = jnp.sum(gram * identity, axis=0, keepdims=True)
    return inverse * (jnp.sqrt(diagonal) / jnp.sqrt(frobenius))


def transform_kernel(gram_ref, v_ref, half, mid, full, core_slot, y_slot, x_slot, send, recv):
    row, z = lax.axis_index("row"), lax.axis_index("pair")
    core = lax.rem(row, 2)
    y = lax.rem(lax.div(row, 2), 4)
    x = lax.div(row, 8)
    other = row + 1 - 2 * core
    y_peers = [x * 8 + lax.rem(y + k, 4) * 2 + core for k in (1, 2, 3)]
    x_peers = [lax.rem(x + k, 4) * 8 + y * 2 + core for k in (1, 2, 3)]
    barrier = pltpu.get_barrier_semaphore()
    for peer in [other] + y_peers + x_peers:
        pl.semaphore_signal(barrier, inc=1, device_id=(peer, z), device_id_type=MESH)
    pl.semaphore_wait(barrier, 7)

    h = gram_ref.shape[0] // 2
    mine = pl.ds(pl.multiple_of(core * h, h), h)
    theirs = pl.ds(pl.multiple_of((1 - core) * h, h), h)

    def copy(src, dst, slot, peer):
        return pltpu.make_async_remote_copy(
            src_ref=src, dst_ref=dst, send_sem=send.at[slot], recv_sem=recv.at[slot],
            device_id=(peer, z), device_id_type=MESH,
        )

    first = copy(gram_ref.at[theirs], core_slot, 0, other)
    first.start()
    first.wait_recv()
    half[...] = gram_ref[mine] + core_slot[...]
    y_copies = [copy(half, y_slot.at[k], 1 + k, y_peers[k]) for k in range(3)]
    for c in y_copies:
        c.start()
    total = half[...]
    for k, c in enumerate(y_copies):
        c.wait_recv()
        total = total + y_slot[k]
    mid[...] = total
    x_copies = [copy(mid, x_slot.at[k], 4 + k, x_peers[k]) for k in range(3)]
    for c in x_copies:
        c.start()
    for k, c in enumerate(x_copies):
        c.wait_recv()
        total = total + x_slot[k]
    full[mine] = total
    last = copy(full.at[mine], full.at[mine], 7, other)
    last.start()
    last.wait_recv()
    v_ref[...] = orthogonalizer(full[...])
    for c in [first] + y_copies + x_copies + [last]:
        c.wait_send()


def transform(gram):
    n = gram.shape[0]
    h = n // 2
    vmem = pl.BlockSpec(memory_space=pltpu.VMEM)
    return pl.pallas_call(
        transform_kernel,
        out_shape=jax.ShapeDtypeStruct((n, n), jnp.float32),
        in_specs=[vmem],
        out_specs=vmem,
        scratch_shapes=[
            pltpu.VMEM((h, n), jnp.float32),
            pltpu.VMEM((h, n), jnp.float32),
            pltpu.VMEM((n, n), jnp.float32),
            pltpu.VMEM((h, n), jnp.float32),
            pltpu.VMEM((3, h, n), jnp.float32),
            pltpu.VMEM((3, h, n), jnp.float32),
            pltpu.SemaphoreType.DMA((8,)),
            pltpu.SemaphoreType.DMA((8,)),
        ],
        compiler_params=pltpu.CompilerParams(collective_id=0, has_side_effects=True),
        name="transform",
    )(gram)


def partner_2(value, axis, stride):
    mask = 2**stride
    pairs = [(source, source ^ mask) for source in range(lax.axis_size(axis))]
    return lax.ppermute(value, axis, pairs)


def swap_branch(bit_index):
    def apply_swap(folded):
        return partner_2(folded, "pair", bit_index)

    return apply_swap


def body(matrix, partner):
    rows_here, width = matrix.shape
    half_width = width // 2
    pair_count = lax.axis_size("pair")
    bit_total = pair_count.bit_length() - 1
    my_pair = lax.axis_index("pair")
    columns = matrix
    for round_index in range(ROUNDS):
        rotation = transform(dot(columns.T, columns))
        columns = dot(columns, rotation)
        if round_index + 1 < ROUNDS:
            offset = jnp.bitwise_xor(partner[round_index, my_pair], my_pair)
            folded = columns[:, half_width:].reshape(rows_here // 2, width)
            positions = jnp.arange(bit_total, dtype=jnp.int32)
            which_bit = jnp.sum(jnp.bitwise_and(jnp.right_shift(offset, positions), 1) * positions)
            folded = lax.switch(
                which_bit, [swap_branch(bit_index) for bit_index in range(bit_total)], folded
            )
            second = folded.reshape(rows_here, half_width)
            columns = jnp.concatenate([columns[:, :half_width], second], axis=1)
    return columns


def solution(mesh):
    in_specs = (P("row", "pair"), P())
    out_specs = P("row", "pair")
    return jax.shard_map(body, mesh=mesh, in_specs=in_specs, out_specs=out_specs, check_vma=False)
```

time: 724 us -> 251 us (0.35)
  waiting for transfers between devices: 615 us -> 108 us
  Pallas kernels: 0 us -> 72.9 us
  between operations: 20.8 us -> 3.87 us
  matrix products: 27 us -> 16.7 us
    psum x4 -> x0, waiting for transfers between devices: 542 us -> none  [full_gram(): return lax.psum(local_gram, 'row')]
    pallas_call x0 -> x4, Pallas kernels: none -> 72.9 us  [transform(): pl.pallas_call(transform_kernel, out_shape=jax.ShapeDtypeStruct((n, n), j...]
    ppermute x3, waiting for transfers between devices: 73.4 us -> 108 us  [partner_2(): return lax.ppermute(value, axis, pairs)]
    dot_general x76 -> x8, matrix products: 27 us -> 16.7 us  [dot(): return jnp.dot(a, b, precision=HIGHEST, preferred_element_type=jnp.float32)]
  transfers between devices with their start and end apart: 7 -> 3, of which waited for: 7 -> 3; matrix products, arithmetic and copies ran while one was open for 0% -> 0% of each run, Pallas kernels for 0% -> 0%
where the time goes in v1:
time: 251 us; the launch traced here: 250 us
  waiting for transfers between devices  108 us (43%)
  Pallas kernels  72.9 us (29%)
  starting transfers between devices  25.2 us (10%)
  local copies, waits for them, and re-layouts  21.2 us (8%)
  matrix products  16.7 us (7%)
  between operations  3.87 us (2%)
    ppermute x3, waiting for transfers between devices, partner_2(): return lax.ppermute(value, axis, pairs)  108 us
    pallas_call x4, Pallas kernels, transform(): pl.pallas_call(transform_kernel, out_shape=jax.ShapeDtypeStruct((n, n), j...  72.9 us
    ppermute x3, starting transfers between devices, partner_2(): return lax.ppermute(value, axis, pairs)  25.2 us
    dot_general x8, matrix products, dot(): return jnp.dot(a, b, precision=HIGHEST, preferred_element_type=jnp.float32)  16.7 us
  transfers between devices with their start and end apart: 3, of which 3 were waited for; matrix products, arithmetic and copies ran while one was open for 0% of the time, Pallas kernels for 0%

profile of v1, /device:TPU:1, one launch (start us, length us, event | category | flops | bytes accessed | tf_op | source)
XLA Modules:
  0.0 250.3 jit_solution(7129803043930746456)
XLA Ops:
  7.1 2.5 fusion.12.gram_ref
  9.5 19.8 %transform.4 = f32[128,128]{1,0:T(8,128)} custom-call(f32[128,128]{1,0:T(8,128)} %fusion.12.gram_ref), custom_call_target="tpu_custom_call" | custom-call | tf_op jit(solution)/shard_map/transform/pallas_call | solution.py:93
  29.4 1.9 convolution_bitcast_fusion
  31.3 34.8 %conditional.3 = (f32[2048,64]{0,1:T(8,128)S(1)}) conditional(s32[]{:T(128)} %clamp.9, (f32[2048,128]{0,1:T(8,128)S(1)}) %tuple.57, (f32[2048,128]{0,1:T(8,128)S(1)}) %tuple.57, (f32[2048,128]{0,1:T(8,128)S(1)}) %tuple.57, (f32[2048,128]{0,1:T(8,128)S(1)}) %tuple.57), branch_computations={%region_1.0_spmd, %region_2.0_spmd, %region_3.0_spmd, %region_4.0_... | conditional | bytes 8388656 | solution.py:141
  32.6 1.6 slice.52
  35.2 4.9 %collective-permute-start.1 = (f32[1024,128]{1,0:T(8,128)}, f32[1024,128]{1,0:T(8,128)S(1)}, u32[]{:S(2)}, u32[]{:S(2)}) collective-permute-start(f32[1024,128]{1,0:T(8,128)} %reshape.80), channel_id=1, source_target_pairs={{0,2},{1,3},{2,0},{3,1},{4,6},{5,7},{6,4},{7,5},{8,10},{9,11},{10,... | collective-permute-start | bytes 1572872 | tf_op jit(solution)/shard_map/cond/branch_1_fun/ppermute | solution.py:116
  40.1 23.1 %collective-permute-done.1 = f32[1024,128]{1,0:T(8,128)S(1)} collective-permute-done((f32[1024,128]{1,0:T(8,128)}, f32[1024,128]{1,0:T(8,128)S(1)}, u32[]{:S(2)}, u32[]{:S(2)}) %collective-permute-start.1) | collective-permute-done | bytes 524320 | tf_op jit(solution)/shard_map/cond/branch_1_fun/ppermute | solution.py:116
  66.2 1.6 fusion.5.gram_ref
  67.8 19.2 %transform.5 = f32[128,128]{1,0:T(8,128)} custom-call(f32[128,128]{1,0:T(8,128)} %fusion.5.gram_ref), custom_call_target="tpu_custom_call" | custom-call | tf_op jit(solution)/shard_map/transform/pallas_call | solution.py:93
  87.0 1.9 fusion.4
  88.9 59.6 %conditional.4 = (f32[2048,64]{0,1:T(8,128)S(1)}) conditional(s32[]{:T(128)} %clamp.10, (f32[2048,128]{0,1:T(8,128)S(1)}) %tuple.62, (f32[2048,128]{0,1:T(8,128)S(1)}) %tuple.62, (f32[2048,128]{0,1:T(8,128)S(1)}) %tuple.62, (f32[2048,128]{0,1:T(8,128)S(1)}) %tuple.62), branch_computations={%region_6.0_spmd, %region_7.0_spmd, %region_8.0_spmd, %region_9.0_... | conditional | bytes 8388656 | solution.py:141
  90.2 1.6 slice.57
  92.8 7.6 %collective-permute-start.6 = (f32[1024,128]{1,0:T(8,128)}, f32[1024,128]{1,0:T(8,128)S(1)}, u32[]{:S(2)}, u32[]{:S(2)}) collective-permute-start(f32[1024,128]{1,0:T(8,128)} %reshape.90), channel_id=1, source_target_pairs={{0,4},{1,5},{2,6},{3,7},{4,0},{5,1},{6,2},{7,3},{8,12},{9,13},{10,... | collective-permute-start | bytes 1572872 | tf_op jit(solution)/shard_map/cond/branch_2_fun/ppermute | solution.py:116
  100.4 45.4 %collective-permute-done.6 = f32[1024,128]{1,0:T(8,128)S(1)} collective-permute-done((f32[1024,128]{1,0:T(8,128)}, f32[1024,128]{1,0:T(8,128)S(1)}, u32[]{:S(2)}, u32[]{:S(2)}) %collective-permute-start.6) | collective-permute-done | bytes 524320 | tf_op jit(solution)/shard_map/cond/branch_2_fun/ppermute | solution.py:116
  148.6 1.6 fusion.3.gram_ref
  150.2 16.5 %transform.6 = f32[128,128]{1,0:T(8,128)} custom-call(f32[128,128]{1,0:T(8,128)} %fusion.3.gram_ref), custom_call_target="tpu_custom_call" | custom-call | tf_op jit(solution)/shard_map/transform/pallas_call | solution.py:93
  166.7 1.9 fusion.2
  168.6 59.0 %conditional.5 = (f32[2048,64]{0,1:T(8,128)S(1)}) conditional(s32[]{:T(128)} %clamp.11, (f32[2048,128]{0,1:T(8,128)S(1)}) %tuple.67, (f32[2048,128]{0,1:T(8,128)S(1)}) %tuple.67, (f32[2048,128]{0,1:T(8,128)S(1)}) %tuple.67, (f32[2048,128]{0,1:T(8,128)S(1)}) %tuple.67), branch_computations={%region_11.0_spmd, %region_12.0_spmd, %region_13.0_spmd, %region_1... | conditional | bytes 8388656 | solution.py:141
  170.2 1.6 slice.62
  172.8 12.7 %collective-permute-start.11 = (f32[1024,128]{1,0:T(8,128)}, f32[1024,128]{1,0:T(8,128)S(1)}, u32[]{:S(2)}, u32[]{:S(2)}) collective-permute-start(f32[1024,128]{1,0:T(8,128)} %reshape.100), channel_id=1, source_target_pairs={{0,8},{1,9},{2,10},{3,11},{4,12},{5,13},{6,14},{7,15},{8,0},{9,1},... | collective-permute-start | bytes 1572872 | tf_op jit(solution)/shard_map/cond/branch_3_fun/ppermute | solution.py:116
  185.5 39.4 %collective-permute-done.11 = f32[1024,128]{1,0:T(8,128)S(1)} collective-permute-done((f32[1024,128]{1,0:T(8,128)}, f32[1024,128]{1,0:T(8,128)S(1)}, u32[]{:S(2)}, u32[]{:S(2)}) %collective-permute-start.11) | collective-permute-done | bytes 524320 | tf_op jit(solution)/shard_map/cond/branch_3_fun/ppermute | solution.py:116
  227.7 1.6 fusion.1.gram_ref
  229.3 17.3 %transform.7 = f32[128,128]{1,0:T(8,128)} custom-call(f32[128,128]{1,0:T(8,128)} %fusion.1.gram_ref), custom_call_target="tpu_custom_call" | custom-call | tf_op jit(solution)/shard_map/transform/pallas_call | solution.py:93
  246.7 3.6 %fusion = f32[2048,128]{1,0:T(8,128)} fusion(f32[128,128]{1,0:T(8,128)} %transform.7, f32[2048,64]{0,1:T(8,128)S(1)} %get-tuple-element.69, f32[2048,64]{0,1:T(8,128)S(1)} %slice.65), kind=kOutput, calls=%fused_computation.4 | convolution fusion | flops 402915328 | bytes 2162688 | tf_op jit(solution)/shard_map/dot_general | solution.py:17
  (23 shorter events, 18.5 us)
Async XLA Ops:
  0.0 7.1 %copy-start = (f32[2048,128]{1,0:T(8,128)S(1)}, f32[2048,128]{1,0:T(8,128)}, u32[]{:S(2)}) copy-start(f32[2048,128]{1,0:T(8,128)} %param.14) | copy-start | bytes 3145732
  0.0 0.8 copy-start.1
  35.2 28.0 %collective-permute-start.1 = (f32[1024,128]{1,0:T(8,128)}, f32[1024,128]{1,0:T(8,128)S(1)}, u32[]{:S(2)}, u32[]{:S(2)}) collective-permute-start(f32[1024,128]{1,0:T(8,128)} %reshape.80), channel_id=1, source_target_pairs={{0,2},{1,3},{2,0},{3,1},{4,6},{5,7},{6,4},{7,5},{8,10},{9,11},{10,... | collective-permute-start | bytes 1572872 | tf_op jit(solution)/shard_map/cond/branch_1_fun/ppermute | solution.py:116
  92.8 53.0 %collective-permute-start.6 = (f32[1024,128]{1,0:T(8,128)}, f32[1024,128]{1,0:T(8,128)S(1)}, u32[]{:S(2)}, u32[]{:S(2)}) collective-permute-start(f32[1024,128]{1,0:T(8,128)} %reshape.90), channel_id=1, source_target_pairs={{0,4},{1,5},{2,6},{3,7},{4,0},{5,1},{6,2},{7,3},{8,12},{9,13},{10,... | collective-permute-start | bytes 1572872 | tf_op jit(solution)/shard_map/cond/branch_2_fun/ppermute | solution.py:116
  172.8 52.2 %collective-permute-start.11 = (f32[1024,128]{1,0:T(8,128)}, f32[1024,128]{1,0:T(8,128)S(1)}, u32[]{:S(2)}, u32[]{:S(2)}) collective-permute-start(f32[1024,128]{1,0:T(8,128)} %reshape.100), channel_id=1, source_target_pairs={{0,8},{1,9},{2,10},{3,11},{4,12},{5,13},{6,14},{7,15},{8,0},{9,1},... | collective-permute-start | bytes 1572872 | tf_op jit(solution)/shard_map/cond/branch_3_fun/ppermute | solution.py:116

commit v2 on v0

v2 whole, which is shorter than its diff:
```python
import functools

import jax
import jax.numpy as jnp
from jax import lax
from jax.experimental import pallas as pl
from jax.experimental.pallas import tpu as pltpu
from jax.sharding import PartitionSpec as P

ROUNDS = 4
NS_ITERS = 6
CHUNKS = 8
MESH = pl.DeviceIdType.MESH
HIGHEST = lax.Precision.HIGHEST
F32 = jnp.float32

OFFSETS = sorted(
    [(dx, dy) for dx in range(4) for dy in range(4) if dx or dy],
    key=lambda d: -(min(d[0], 4 - d[0]) + min(d[1], 4 - d[1])),
)


def dot(a, b):
    return jnp.dot(a, b, precision=HIGHEST, preferred_element_type=F32)


def dot_t(a, b):
    return lax.dot_general(
        a, b, (((0,), (0,)), ((), ())), precision=HIGHEST, preferred_element_type=F32
    )


def low_lanes(shape, half):
    return lax.broadcasted_iota(jnp.int32, shape, 1) < half


def orthogonalizer(gram, both, corr):
    size = gram.shape[0]
    rows = lax.broadcasted_iota(jnp.int32, (size, size), 0)
    cols = lax.broadcasted_iota(jnp.int32, (size, size), 1)
    identity = jnp.where(rows == cols, 1.0, 0.0).astype(F32)
    square_sum = jnp.sum(jnp.sum(gram * gram, axis=0, keepdims=True), axis=1, keepdims=True)
    frobenius = jnp.sqrt(square_sum)
    root = gram / frobenius
    inverse = 1.5 * identity - 0.5 * root
    root = dot(root, inverse)

    both[:size] = root
    both[size:] = inverse

    def step(_, carry):
        corr[...] = 1.5 * identity - 0.5 * dot(both[size:], both[:size])
        both[...] = dot(both[...], corr[...])
        return carry

    lax.fori_loop(0, NS_ITERS - 2, step, 0)
    inverse = dot(both[size:], 1.5 * identity - 0.5 * dot(both[size:], both[:size]))
    diagonal = jnp.sum(gram * identity, axis=0, keepdims=True)
    return inverse * (jnp.sqrt(diagonal) / jnp.sqrt(frobenius))


def diagonal_blocks(gram_e, gram_s):
    h = gram_e.shape[0] // 2
    low = low_lanes((h, 2 * h), h)
    a = jnp.where(low, gram_e[:h], gram_e[h:])
    b = jnp.where(low, gram_s[:h], gram_s[h:])
    a = a + pltpu.roll(a, h, 1)
    b = b + pltpu.roll(b, h, 1)
    return jnp.where(low, a, b)


def cross_block(product):
    h = product.shape[0] // 2
    c = jnp.where(low_lanes((h, 2 * h), h), product[h:], product[:h])
    c = c + pltpu.roll(c, h, 1)
    q = h // 2
    return jnp.where(low_lanes((q, 2 * h), h), c[:q], c[q:])


def assemble(diagonal, cross):
    h = diagonal.shape[0]
    low = low_lanes((h, 2 * h), h)
    zero = jnp.zeros((h, 2 * h), F32)
    c = jnp.concatenate([pltpu.roll(cross, h, 1), cross], axis=0)
    upper = jnp.concatenate([jnp.where(low, 0.0, c), zero], axis=0)
    blocks = jnp.concatenate(
        [jnp.where(low, diagonal, 0.0), jnp.where(low, 0.0, diagonal)], axis=0
    )
    return blocks + upper + upper.T


class Place:
    def __init__(self):
        self.row, self.z = lax.axis_index("row"), lax.axis_index("pair")
        self.core = lax.rem(self.row, 2)
        y = lax.rem(lax.div(self.row, 2), 4)
        x = lax.div(self.row, 8)
        self.other = self.row + 1 - 2 * self.core
        self.peers = [
            (lax.rem(x + dx, 4) * 4 + lax.rem(y + dy, 4)) * 2 + self.core for dx, dy in OFFSETS
        ]

    def greet(self, more=()):
        barrier = pltpu.get_barrier_semaphore()
        targets = [(r, self.z) for r in self.peers + [self.other]] + [(self.row, p) for p in more]
        for target in targets:
            pl.semaphore_signal(barrier, inc=1, device_id=target, device_id_type=MESH)
        return lambda: pl.semaphore_wait(barrier, len(targets))

    def half(self, ref_rows):
        h = ref_rows // 2
        return (
            pl.ds(pl.multiple_of(self.core * h, h), h),
            pl.ds(pl.multiple_of((1 - self.core) * h, h), h),
        )


def copy(src, dst, send, recv, target):
    return pltpu.make_async_remote_copy(
        src_ref=src, dst_ref=dst, send_sem=send, recv_sem=recv,
        device_id=target, device_id_type=MESH,
    )


def exchange(place, src, slots, send, recv, base):
    copies = [
        copy(src, slots.at[k], send.at[base + k], recv.at[base + k], (peer, place.z))
        for k, peer in enumerate(place.peers)
    ]
    for c in copies:
        c.start()
    return copies


def collect(copies, slots, total):
    for k in reversed(range(len(copies))):
        copies[k].wait_recv()
        total = total + slots[k]
    return total


def split_sum(place, local, half, slot, slots, result, send, recv, base):
    mine, theirs = place.half(local.shape[0])
    first = copy(local.at[theirs], slot, send.at[base], recv.at[base], (place.other, place.z))
    first.start()
    first.wait_recv()
    half[...] = local[mine] + slot[...]
    copies = exchange(place, half, slots, send, recv, base + 1)
    result[mine] = collect(copies, slots, half[...])
    last = copy(
        result.at[mine], result.at[mine], send.at[base + 16], recv.at[base + 16],
        (place.other, place.z),
    )
    last.start()
    last.wait_recv()
    return [first] + copies + [last]


def start_kernel(x_ref, e_ref, s_ref, g_ref, local, half, slot, slots, result, send, recv):
    place = Place()
    wait = place.greet()
    n, w = x_ref.shape
    n, h = n // 2, w // 2
    m = n // 4
    low = low_lanes((m, w), h)

    def square(c, grams):
        rows = pl.ds(pl.multiple_of(c * m, m), m)
        top = x_ref[rows]
        bottom = pltpu.roll(x_ref[pl.ds(pl.multiple_of(n + c * m, m), m)], h, 1)
        e, s = jnp.where(low, top, bottom), jnp.where(low, bottom, top)
        e_ref[rows] = e
        s_ref[rows] = s
        return grams[0] + dot_t(e, e), grams[1] + dot_t(s, s), grams[2] + dot_t(e, s)

    zero = jnp.zeros((w, w), F32)
    ee, ss, es = lax.fori_loop(0, 4, square, (zero, zero, zero))
    local[:h] = diagonal_blocks(ee, ss)
    local[h:] = cross_block(es)
    wait()
    copies = split_sum(place, local, half, slot, slots, result, send, recv, 0)
    g_ref[...] = assemble(result[:h], result[h:])
    for c in copies:
        c.wait_send()


def block_form(v):
    h = v.shape[0] // 2
    low = low_lanes((h, 2 * h), h)
    va, vb = v[:h], v[h:]
    ra, rb = pltpu.roll(va, h, 1), pltpu.roll(vb, h, 1)
    left = [jnp.where(low, va, 0.0), jnp.where(low, 0.0, ra), jnp.where(low, 0.0, rb), jnp.where(low, vb, 0.0)]
    right = [jnp.where(low, 0.0, va), jnp.where(low, ra, 0.0), jnp.where(low, rb, 0.0), jnp.where(low, 0.0, vb)]
    return jnp.concatenate(
        [jnp.concatenate(left, axis=0), jnp.concatenate(right, axis=0)], axis=1
    )


def round_kernel(
    stride, p_ref, q_ref, g_ref, e_ref, r_ref, gout_ref,
    s_ref, w_ref, dlocal, dhalf, dslot, dslots, dresult, dother, clocal, cslot, csum, cslots,
    bsend, brecv, send, recv, both, corr,
):
    place = Place()
    bit = lax.rem(lax.div(place.z, stride), 2)
    partner = place.z + stride * (1 - 2 * bit)
    wait = place.greet([partner])
    n, w = p_ref.shape
    h, m = w // 2, n // CHUNKS
    across = (place.row, partner)

    w_ref[...] = block_form(orthogonalizer(g_ref[...], both, corr))
    wait()

    def bulk(c):
        rows = pl.ds(pl.multiple_of(c * m, m), m)
        return rows, copy(s_ref.at[rows], r_ref.at[rows], bsend.at[c], brecv.at[c], across)

    def give(c, _):
        rows, out = bulk(c)
        es = dot(jnp.concatenate([p_ref[rows], q_ref[rows]], axis=1), w_ref[...])
        s_ref[rows] = es[:, w:]
        out.start()
        e_ref[rows] = es[:, :w]
        return 0

    lax.fori_loop(0, CHUNKS, give, 0)

    def square(c, grams):
        rows = pl.ds(pl.multiple_of(c * 2 * m, 2 * m), 2 * m)
        e, s = e_ref[rows], s_ref[rows]
        return grams[0] + dot_t(e, e), grams[1] + dot_t(s, s)

    zero = jnp.zeros((w, w), F32)
    dlocal[...] = diagonal_blocks(*lax.fori_loop(0, CHUNKS // 2, square, (zero, zero)))
    copies = split_sum(place, dlocal, dhalf, dslot, dslots, dresult, send, recv, 0)
    ours = copy(dresult, dother, send.at[17], recv.at[17], across)
    ours.start()

    def take(c, total):
        rows, out = bulk(c)
        out.wait_recv()
        return total + dot_t(e_ref[rows], r_ref[rows])

    product = lax.fori_loop(0, CHUNKS, take, zero)
    clocal[...] = cross_block(product)
    first = copy(clocal, cslot, send.at[18], recv.at[18], (place.other, place.z))
    first.start()
    first.wait_recv()
    csum[...] = clocal[...] + cslot[...]
    more = exchange(place, csum, cslots, send, recv, 19)
    cross = collect(more, cslots, csum[...])
    ours.wait_recv()
    diagonal = jnp.where(low_lanes((h, w), h), dresult[...], dother[...])
    gout_ref[...] = assemble(diagonal, cross)

    def sent(c, _):
        bulk(c)[1].wait_send()
        return 0

    lax.fori_loop(0, CHUNKS, sent, 0)
    for c in copies + [ours, first] + more:
        c.wait_send()


def last_kernel(p_ref, q_ref, g_ref, out_ref, w_ref, both, corr):
    n, w = p_ref.shape
    w_ref[...] = block_form(orthogonalizer(g_ref[...], both, corr))
    h = w // 2
    m = n // CHUNKS
    low = low_lanes((m, w), h)

    def write(c, _):
        rows = pl.ds(pl.multiple_of(c * m, m), m)
        es = dot(jnp.concatenate([p_ref[rows], q_ref[rows]], axis=1), w_ref[...])
        e, s = es[:, :w], es[:, w:]
        out_ref[rows] = jnp.where(low, e, s)
        out_ref[pl.ds(pl.multiple_of(n + c * m, m), m)] = pltpu.roll(jnp.where(low, s, e), h, 1)
        return 0

    lax.fori_loop(0, CHUNKS, write, 0)


def body(matrix, partner):
    rows_here, width = matrix.shape
    n, h, q = rows_here // 2, width // 2, width // 4
    bit_total = lax.axis_size("pair").bit_length() - 1
    my_pair = lax.axis_index("pair")
    vmem = pl.BlockSpec(memory_space=pltpu.VMEM)
    dma = pltpu.SemaphoreType.DMA
    tall = jax.ShapeDtypeStruct((n, width), F32)
    square = jax.ShapeDtypeStruct((width, width), F32)

    def buf(*shape):
        return pltpu.VMEM(shape, F32)

    start = pl.pallas_call(
        start_kernel,
        out_shape=(tall, tall, square),
        in_specs=[vmem],
        out_specs=(vmem, vmem, vmem),
        scratch_shapes=[
            buf(h + q, width), buf((h + q) // 2, width), buf((h + q) // 2, width),
            buf(15, (h + q) // 2, width), buf(h + q, width), dma((17,)), dma((17,)),
        ],
        compiler_params=pltpu.CompilerParams(collective_id=8, has_side_effects=True, vmem_limit_bytes=32 << 20),
        name="start",
    )

    def turn(bit):
        return pl.pallas_call(
            functools.partial(round_kernel, 2**bit),
            out_shape=(tall, tall, square),
            in_specs=[vmem] * 3,
            out_specs=(vmem, vmem, vmem),
            scratch_shapes=[
                buf(n, width), buf(2 * width, 2 * width),
                buf(h, width), buf(q, width), buf(q, width), buf(15, q, width), buf(h, width), buf(h, width),
                buf(q, width), buf(q, width), buf(q, width), buf(15, q, width),
                dma((CHUNKS,)), dma((CHUNKS,)), dma((34,)), dma((34,)), buf(2 * width, width), buf(width, width),
            ],
            compiler_params=pltpu.CompilerParams(collective_id=bit, has_side_effects=True, vmem_limit_bytes=32 << 20),
            name=f"turn{bit}",
        )

    last = pl.pallas_call(
        last_kernel,
        out_shape=jax.ShapeDtypeStruct((rows_here, width), F32),
        in_specs=[vmem] * 3,
        out_specs=vmem,
        scratch_shapes=[buf(2 * width, 2 * width), buf(2 * width, width), buf(width, width)],
        compiler_params=pltpu.CompilerParams(vmem_limit_bytes=32 << 20),
        name="last",
    )

    turns = [turn(bit) for bit in range(bit_total)]
    offsets = jnp.bitwise_xor(partner[:, my_pair], my_pair)
    bits = jnp.sum(
        jnp.stack([(jnp.bitwise_and(jnp.right_shift(offsets, b), 1) * b) for b in range(bit_total)]), axis=0
    )
    state = start(matrix)
    for round_index in range(ROUNDS - 1):
        state = lax.switch(bits[round_index], turns, *state)
    return last(*state)


def solution(mesh):
    in_specs = (P("row", "pair"), P())
    out_specs = P("row", "pair")
    return jax.shard_map(body, mesh=mesh, in_specs=in_specs, out_specs=out_specs, check_vma=False)
```

time: 724 us -> 194 us (0.27)
  the two profiles are of different devices: /device:TPU:1 before, /device:TPU:33 now
where the time goes in v2:
time: 194 us
  Pallas kernels  189 us (97%)
  local copies, waits for them, and re-layouts  2.49 us (1%)
  between operations  1.96 us (1%)
    pallas_call x3, Pallas kernels, body(): state = lax.switch(bits[round_index], turns, *state)  166 us
    pallas_call x1, Pallas kernels, body(): state = start(matrix)  15.8 us
    pallas_call x1, Pallas kernels, body(): return last(*state)  6.68 us

profile of v2, /device:TPU:33, one launch (start us, length us, event | category | flops | bytes accessed | tf_op | source)
XLA Modules:
  0.0 193.5 jit_solution(11353782144388983674)
XLA Ops:
  0.0 0.0 copy-start.1
  0.0 0.7 copy-done.1
  0.7 0.1 add_add_fusion
  0.8 0.6 fusion
  3.3 0.0 copy-start
  3.3 1.2 copy-done
  4.5 15.8 %start.1 = (f32[1024,128]{1,0:T(8,128)S(1)}, f32[1024,128]{1,0:T(8,128)S(1)}, f32[128,128]{1,0:T(8,128)S(1)}) custom-call(f32[2048,128]{1,0:T(8,128)S(1)} %copy-done), custom_call_target="tpu_custom_call" | custom-call | tf_op jit(solution)/shard_map/start/pallas_call | solution.py:341
  20.3 73.2 %conditional.3 = ((f32[1024,128]{1,0:T(8,128)S(1)}, f32[1024,128]{1,0:T(8,128)S(1)}, f32[128,128]{1,0:T(8,128)S(1)})) conditional(s32[]{:T(128)} %bitcast.2, (f32[1024,128]{1,0:T(8,128)S(1)}, f32[1024,128]{1,0:T(8,128)S(1)}, f32[128,128]{1,0:T(8,128)S(1)}) %start.1, (f32[1024,128]{1,0:T(8,128)S(1)}, ...), branch_computations={%region_0.0_spmd, %region_1.0_spmd, %region_2.0_spmd, %region_3.0_... | conditional | bytes 8 | solution.py:343
  20.4 73.2 %turn3.3 = (f32[1024,128]{1,0:T(8,128)S(1)}, f32[1024,128]{1,0:T(8,128)S(1)}, f32[128,128]{1,0:T(8,128)S(1)}) custom-call(f32[1024,128]{1,0:T(8,128)S(1)} %get-tuple-element.86.p_ref, f32[1024,128]{1,0:T(8,128)S(1)} %get-tuple-element.87.q_ref, f32[128,128]{1,0:T(8,128)S(1)} %get-tuple-element.88.g_ref), custom_call_target="tpu_custom_call" | custom-call | tf_op jit(solution)/shard_map/cond/branch_3_fun/turn3/pallas_call | solution.py:343
  93.5 28.0 %conditional.4 = ((f32[1024,128]{1,0:T(8,128)S(1)}, f32[1024,128]{1,0:T(8,128)S(1)}, f32[128,128]{1,0:T(8,128)S(1)})) conditional(s32[]{:T(128)} %bitcast.1, (f32[1024,128]{1,0:T(8,128)S(1)}, f32[1024,128]{1,0:T(8,128)S(1)}, f32[128,128]{1,0:T(8,128)S(1)}) %get-tuple-element.158, (f32[1024,128]{1,0:T(8,128)S(1)}, ...), branch_computations={%region_4.0_spmd, %region_5.0_spmd, %region_6.0_spmd, %region_7.0_... | conditional | bytes 8 | solution.py:343
  93.6 27.8 %turn1.4 = (f32[1024,128]{1,0:T(8,128)S(1)}, f32[1024,128]{1,0:T(8,128)S(1)}, f32[128,128]{1,0:T(8,128)S(1)}) custom-call(f32[1024,128]{1,0:T(8,128)S(1)} %get-tuple-element.92.p_ref, f32[1024,128]{1,0:T(8,128)S(1)} %get-tuple-element.93.q_ref, f32[128,128]{1,0:T(8,128)S(1)} %get-tuple-element.94.g_ref), custom_call_target="tpu_custom_call" | custom-call | tf_op jit(solution)/shard_map/cond/branch_1_fun/turn1/pallas_call | solution.py:343
  121.5 65.3 %conditional.5 = ((f32[1024,128]{1,0:T(8,128)S(1)}, f32[1024,128]{1,0:T(8,128)S(1)}, f32[128,128]{1,0:T(8,128)S(1)})) conditional(s32[]{:T(128)} %bitcast, (f32[1024,128]{1,0:T(8,128)S(1)}, f32[1024,128]{1,0:T(8,128)S(1)}, f32[128,128]{1,0:T(8,128)S(1)}) %get-tuple-element.159, (f32[1024,128]{1,0:T(8,128)S(1)}, ...), branch_computations={%region_8.0_spmd, %region_9.0_spmd, %region_10.0_spmd, %region_11.... | conditional | bytes 8 | solution.py:343
  121.6 65.3 %turn3.5 = (f32[1024,128]{1,0:T(8,128)S(1)}, f32[1024,128]{1,0:T(8,128)S(1)}, f32[128,128]{1,0:T(8,128)S(1)}) custom-call(f32[1024,128]{1,0:T(8,128)S(1)} %get-tuple-element.110.p_ref, f32[1024,128]{1,0:T(8,128)S(1)} %get-tuple-element.111.q_ref, f32[128,128]{1,0:T(8,128)S(1)} %get-tuple-element.112.g_ref), custom_call_target="tpu_custom_call" | custom-call | tf_op jit(solution)/shard_map/cond/branch_3_fun/turn3/pallas_call | solution.py:343
  186.8 6.7 %last.1 = f32[2048,128]{1,0:T(8,128)} custom-call(f32[1024,128]{1,0:T(8,128)S(1)} %get-tuple-element.116.p_ref, f32[1024,128]{1,0:T(8,128)S(1)} %get-tuple-element.117.q_ref, f32[128,128]{1,0:T(8,128)S(1)} %get-tuple-element.118.g_ref), custom_call_target="tpu_custom_call" | custom-call | tf_op jit(solution)/shard_map/last/pallas_call | solution.py:344
Async XLA Ops:
  0.0 0.7 copy-start.1
  3.3 1.2 copy-start

commit v3 on v2

--- a/solution.py
+++ b/solution.py
@@ -10,6 +10,8 @@
 ROUNDS = 4
 NS_ITERS = 6
 CHUNKS = 8
+STORES = 4
+LOADS = 2
 MESH = pl.DeviceIdType.MESH
 HIGHEST = lax.Precision.HIGHEST
 F32 = jnp.float32
@@ -34,7 +36,7 @@
     return lax.broadcasted_iota(jnp.int32, shape, 1) < half
 
 
-def orthogonalizer(gram, both, corr):
+def orthogonalizer(gram, pair):
     size = gram.shape[0]
     rows = lax.broadcasted_iota(jnp.int32, (size, size), 0)
     cols = lax.broadcasted_iota(jnp.int32, (size, size), 1)
@@ -43,18 +45,18 @@
     frobenius = jnp.sqrt(square_sum)
     root = gram / frobenius
     inverse = 1.5 * identity - 0.5 * root
-    root = dot(root, inverse)
-
-    both[:size] = root
-    both[size:] = inverse
+    pair[0] = dot(root, inverse)
+    pair[1] = inverse
 
     def step(_, carry):
-        corr[...] = 1.5 * identity - 0.5 * dot(both[size:], both[:size])
-        both[...] = dot(both[...], corr[...])
+        correction = 1.5 * identity - 0.5 * dot(pair[1], pair[0])
+        root, inverse = dot(pair[0], correction), dot(correction, pair[1])
+        pair[0] = root
+        pair[1] = inverse
         return carry
 
     lax.fori_loop(0, NS_ITERS - 2, step, 0)
-    inverse = dot(both[size:], 1.5 * identity - 0.5 * dot(both[size:], both[:size]))
+    inverse = dot(1.5 * identity - 0.5 * dot(pair[1], pair[0]), pair[1])
     diagonal = jnp.sum(gram * identity, axis=0, keepdims=True)
     return inverse * (jnp.sqrt(diagonal) / jnp.sqrt(frobenius))
 
@@ -102,7 +104,7 @@
 
     def greet(self, more=()):
         barrier = pltpu.get_barrier_semaphore()
-        targets = [(r, self.z) for r in self.peers + [self.other]] + [(self.row, p) for p in more]
+        targets = [(self.row, p) for p in more] + [(r, self.z) for r in self.peers + [self.other]]
         for target in targets:
             pl.semaphore_signal(barrier, inc=1, device_id=target, device_id_type=MESH)
         return lambda: pl.semaphore_wait(barrier, len(targets))
@@ -139,48 +141,68 @@
     return total
 
 
-def split_sum(place, local, half, slot, slots, result, send, recv, base):
-    mine, theirs = place.half(local.shape[0])
-    first = copy(local.at[theirs], slot, send.at[base], recv.at[base], (place.other, place.z))
-    first.start()
-    first.wait_recv()
-    half[...] = local[mine] + slot[...]
-    copies = exchange(place, half, slots, send, recv, base + 1)
-    result[mine] = collect(copies, slots, half[...])
-    last = copy(
-        result.at[mine], result.at[mine], send.at[base + 16], recv.at[base + 16],
-        (place.other, place.z),
-    )
-    last.start()
-    last.wait_recv()
-    return [first] + copies + [last]
-
-
-def start_kernel(x_ref, e_ref, s_ref, g_ref, local, half, slot, slots, result, send, recv):
+class SplitSum:
+    def __init__(self, place, local, half, slot, slots, result, send, recv, base):
+        self.place, self.slots, self.half, self.result = place, slots, half, result
+        self.mine, theirs = place.half(local.shape[0])
+        other = (place.other, place.z)
+        first = copy(local.at[theirs], slot, send.at[base], recv.at[base], other)
+        first.start()
+        first.wait_recv()
+        half[...] = local[self.mine] + slot[...]
+        self.copies = exchange(place, half, slots, send, recv, base + 1)
+        rows = result.at[self.mine]
+        self.last = copy(rows, rows, send.at[base + 16], recv.at[base + 16], other)
+        self.all = [first] + self.copies + [self.last]
+
+    def share(self):
+        self.result[self.mine] = collect(self.copies, self.slots, self.half[...])
+        self.last.start()
+
+    def finish(self):
+        self.last.wait_recv()
+
+
+def start_kernel(
+    x_hbm, partner_ref, e_ref, s_ref, g_ref, bit0_ref, bit1_ref, bit2_ref,
+    x_ref, local, half, slot, slots, result, send, recv, load,
+):
+    n, w = e_ref.shape
+    h, m = w // 2, n // LOADS
+    loads = [
+        [
+            pltpu.make_async_copy(x_hbm.at[rows], x_ref.at[rows], load.at[side, c])
+            for side, rows in enumerate((pl.ds(c * m, m), pl.ds(n + c * m, m)))
+        ]
+        for c in range(LOADS)
+    ]
+    for both in loads:
+        for c in both:
+            c.start()
     place = Place()
     wait = place.greet()
-    n, w = x_ref.shape
-    n, h = n // 2, w // 2
-    m = n // 4
+    for round_index, bit_ref in enumerate((bit0_ref, bit1_ref, bit2_ref)):
+        offset = jnp.bitwise_xor(partner_ref[round_index, place.z], place.z)
+        bit_ref[0] = sum(jnp.where(offset >= s, 1, 0) for s in (2, 4, 8))
     low = low_lanes((m, w), h)
-
-    def square(c, grams):
-        rows = pl.ds(pl.multiple_of(c * m, m), m)
-        top = x_ref[rows]
-        bottom = pltpu.roll(x_ref[pl.ds(pl.multiple_of(n + c * m, m), m)], h, 1)
+    ee = ss = es = jnp.zeros((w, w), F32)
+    for c in range(LOADS):
+        for one in loads[c]:
+            one.wait()
+        rows = pl.ds(c * m, m)
+        top, bottom = x_ref[rows], pltpu.roll(x_ref[pl.ds(n + c * m, m)], h, 1)
         e, s = jnp.where(low, top, bottom), jnp.where(low, bottom, top)
         e_ref[rows] = e
         s_ref[rows] = s
-        return grams[0] + dot_t(e, e), grams[1] + dot_t(s, s), grams[2] + dot_t(e, s)
-
-    zero = jnp.zeros((w, w), F32)
-    ee, ss, es = lax.fori_loop(0, 4, square, (zero, zero, zero))
+        ee, ss, es = ee + dot_t(e, e), ss + dot_t(s, s), es + dot_t(e, s)
     local[:h] = diagonal_blocks(ee, ss)
     local[h:] = cross_block(es)
     wait()
-    copies = split_sum(place, local, half, slot, slots, result, send, recv, 0)
+    total = SplitSum(place, local, half, slot, slots, result, send, recv, 0)
+    total.share()
+    total.finish()
     g_ref[...] = assemble(result[:h], result[h:])
-    for c in copies:
+    for c in total.all:
         c.wait_send()
 
 
@@ -199,7 +221,7 @@
 def round_kernel(
     stride, p_ref, q_ref, g_ref, e_ref, r_ref, gout_ref,
     s_ref, w_ref, dlocal, dhalf, dslot, dslots, dresult, dother, clocal, cslot, csum, cslots,
-    bsend, brecv, send, recv, both, corr,
+    bsend, brecv, send, recv, pair,
 ):
     place = Place()
     bit = lax.rem(lax.div(place.z, stride), 2)
@@ -209,7 +231,7 @@
     h, m = w // 2, n // CHUNKS
     across = (place.row, partner)
 
-    w_ref[...] = block_form(orthogonalizer(g_ref[...], both, corr))
+    w_ref[...] = block_form(orthogonalizer(g_ref[...], pair))
     wait()
 
     def bulk(c):
@@ -227,65 +249,91 @@
     lax.fori_loop(0, CHUNKS, give, 0)
 
     def square(c, grams):
-        rows = pl.ds(pl.multiple_of(c * 2 * m, 2 * m), 2 * m)
+        rows = pl.ds(pl.multiple_of(c * m, m), m)
         e, s = e_ref[rows], s_ref[rows]
         return grams[0] + dot_t(e, e), grams[1] + dot_t(s, s)
-
-    zero = jnp.zeros((w, w), F32)
-    dlocal[...] = diagonal_blocks(*lax.fori_loop(0, CHUNKS // 2, square, (zero, zero)))
-    copies = split_sum(place, dlocal, dhalf, dslot, dslots, dresult, send, recv, 0)
-    ours = copy(dresult, dother, send.at[17], recv.at[17], across)
-    ours.start()
 
     def take(c, total):
         rows, out = bulk(c)
         out.wait_recv()
         return total + dot_t(e_ref[rows], r_ref[rows])
 
-    product = lax.fori_loop(0, CHUNKS, take, zero)
-    clocal[...] = cross_block(product)
+    def cross():
+        return cross_block(lax.fori_loop(0, CHUNKS, take, zero))
+
+    zero = jnp.zeros((w, w), F32)
+    dlocal[...] = diagonal_blocks(*lax.fori_loop(0, CHUNKS, square, (zero, zero)))
+    total = SplitSum(place, dlocal, dhalf, dslot, dslots, dresult, send, recv, 0)
+    ours = copy(dresult, dother, send.at[17], recv.at[17], across)
     first = copy(clocal, cslot, send.at[18], recv.at[18], (place.other, place.z))
-    first.start()
+    if stride == 1:
+        clocal[...] = cross()
+        first.start()
+        total.share()
+    else:
+        total.share()
+        total.finish()
+        ours.start()
+        clocal[...] = cross()
+        first.start()
     first.wait_recv()
     csum[...] = clocal[...] + cslot[...]
     more = exchange(place, csum, cslots, send, recv, 19)
-    cross = collect(more, cslots, csum[...])
+    if stride == 1:
+        total.finish()
+        ours.start()
+    summed = collect(more, cslots, csum[...])
     ours.wait_recv()
     diagonal = jnp.where(low_lanes((h, w), h), dresult[...], dother[...])
-    gout_ref[...] = assemble(diagonal, cross)
+    gout_ref[...] = assemble(diagonal, summed)
 
     def sent(c, _):
         bulk(c)[1].wait_send()
         return 0
 
     lax.fori_loop(0, CHUNKS, sent, 0)
-    for c in copies + [ours, first] + more:
+    for c in total.all + [ours, first] + more:
         c.wait_send()
 
 
-def last_kernel(p_ref, q_ref, g_ref, out_ref, w_ref, both, corr):
+def last_kernel(p_ref, q_ref, g_ref, out_hbm, w_ref, pair, out_ref, store):
     n, w = p_ref.shape
-    w_ref[...] = block_form(orthogonalizer(g_ref[...], both, corr))
-    h = w // 2
-    m = n // CHUNKS
+    h, m = w // 2, n // STORES
+    w_ref[...] = block_form(orthogonalizer(g_ref[...], pair))
     low = low_lanes((m, w), h)
+
+    def stores(c):
+        sides = (pl.ds(pl.multiple_of(side * n + c * m, m), m) for side in range(2))
+        return [
+            (rows, pltpu.make_async_copy(out_ref.at[rows], out_hbm.at[rows], store.at[side, c]))
+            for side, rows in enumerate(sides)
+        ]
 
     def write(c, _):
         rows = pl.ds(pl.multiple_of(c * m, m), m)
         es = dot(jnp.concatenate([p_ref[rows], q_ref[rows]], axis=1), w_ref[...])
         e, s = es[:, :w], es[:, w:]
-        out_ref[rows] = jnp.where(low, e, s)
-        out_ref[pl.ds(pl.multiple_of(n + c * m, m), m)] = pltpu.roll(jnp.where(low, s, e), h, 1)
+        (top, to_top), (bottom, to_bottom) = stores(c)
+        out_ref[top] = jnp.where(low, e, s)
+        to_top.start()
+        out_ref[bottom] = pltpu.roll(jnp.where(low, s, e), h, 1)
+        to_bottom.start()
         return 0
 
-    lax.fori_loop(0, CHUNKS, write, 0)
+    lax.fori_loop(0, STORES, write, 0)
+
+    def done(c, _):
+        for _, one in stores(c):
+            one.wait()
+        return 0
+
+    lax.fori_loop(0, STORES, done, 0)
 
 
 def body(matrix, partner):
     rows_here, width = matrix.shape
     n, h, q = rows_here // 2, width // 2, width // 4
     bit_total = lax.axis_size("pair").bit_length() - 1
-    my_pair = lax.axis_index("pair")
     vmem = pl.BlockSpec(memory_space=pltpu.VMEM)
     dma = pltpu.SemaphoreType.DMA
     tall = jax.ShapeDtypeStruct((n, width), F32)
@@ -294,16 +342,20 @@
     def buf(*shape):
         return pltpu.VMEM(shape, F32)
 
+    bit_shape = jax.ShapeDtypeStruct((1,), jnp.int32)
+    smem = pl.BlockSpec(memory_space=pltpu.SMEM)
+    hbm = pl.BlockSpec(memory_space=pltpu.HBM)
+    part = (h + q) // 2
     start = pl.pallas_call(
         start_kernel,
-        out_shape=(tall, tall, square),
-        in_specs=[vmem],
-        out_specs=(vmem, vmem, vmem),
+        out_shape=(tall, tall, square) + (bit_shape,) * 3,
+        in_specs=[hbm, smem],
+        out_specs=(vmem,) * 3 + (smem,) * 3,
         scratch_shapes=[
-            buf(h + q, width), buf((h + q) // 2, width), buf((h + q) // 2, width),
-            buf(15, (h + q) // 2, width), buf(h + q, width), dma((17,)), dma((17,)),
+            buf(rows_here, width), buf(2 * part, width), buf(part, width), buf(part, width),
+            buf(15, part, width), buf(2 * part, width), dma((17,)), dma((17,)), dma((2, LOADS)),
         ],
-        compiler_params=pltpu.CompilerParams(collective_id=8, has_side_effects=True, vmem_limit_bytes=32 << 20),
+        compiler_params=pltpu.CompilerParams(collective_id=8, has_side_effects=True, vmem_limit_bytes=61_800_000),
         name="start",
     )
 
@@ -317,7 +369,7 @@
                 buf(n, width), buf(2 * width, 2 * width),
                 buf(h, width), buf(q, width), buf(q, width), buf(15, q, width), buf(h, width), buf(h, width),
                 buf(q, width), buf(q, width), buf(q, width), buf(15, q, width),
-                dma((CHUNKS,)), dma((CHUNKS,)), dma((34,)), dma((34,)), buf(2 * width, width), buf(width, width),
+                dma((CHUNKS,)), dma((CHUNKS,)), dma((34,)), dma((34,)), buf(2, width, width),
             ],
             compiler_params=pltpu.CompilerParams(collective_id=bit, has_side_effects=True, vmem_limit_bytes=32 << 20),
             name=f"turn{bit}",
@@ -327,20 +379,18 @@
         last_kernel,
         out_shape=jax.ShapeDtypeStruct((rows_here, width), F32),
         in_specs=[vmem] * 3,
-        out_specs=vmem,
-        scratch_shapes=[buf(2 * width, 2 * width), buf(2 * width, width), buf(width, width)],
+        out_specs=hbm,
+        scratch_shapes=[
+            buf(2 * width, 2 * width), buf(2, width, width), buf(rows_here, width), dma((2, STORES)),
+        ],
         compiler_params=pltpu.CompilerParams(vmem_limit_bytes=32 << 20),
         name="last",
     )
 
     turns = [turn(bit) for bit in range(bit_total)]
-    offsets = jnp.bitwise_xor(partner[:, my_pair], my_pair)
-    bits = jnp.sum(
-        jnp.stack([(jnp.bitwise_and(jnp.right_shift(offsets, b), 1) * b) for b in range(bit_total)]), axis=0
-    )
-    state = start(matrix)
-    for round_index in range(ROUNDS - 1):
-        state = lax.switch(bits[round_index], turns, *state)
+    *state, bit0, bit1, bit2 = start(matrix, partner)
+    for bit in (bit0, bit1, bit2):
+        state = lax.switch(bit[0], turns, *state)
     return last(*state)
 
 

time: 194 us -> 186 us (0.959)
  the two profiles are of different devices: /device:TPU:33 before, /device:TPU:1 now
where the time goes in v3:
time: 186 us; the launch traced here: 185 us
  Pallas kernels  183 us (98%)
  between operations  2.07 us (1%)
    pallas_call x3, Pallas kernels, body(): state = lax.switch(bit[0], turns, *state)  158 us
    pallas_call x1, Pallas kernels, body(): *state, bit0, bit1, bit2 = start(matrix, partner)  19.7 us
    pallas_call x1, Pallas kernels, body(): return last(*state)  5.1 us

profile of v3, /device:TPU:1, one launch (start us, length us, event | category | flops | bytes accessed | tf_op | source)
XLA Modules:
  0.0 185.3 jit_solution(14203775648516483398)
XLA Ops:
  0.0 19.7 %start.1 = (f32[1024,128]{1,0:T(8,128)S(1)}, f32[1024,128]{1,0:T(8,128)S(1)}, f32[128,128]{1,0:T(8,128)S(1)}, s32[1]{0:T(128)}, s32[1]{0:T(128)}, /*index=5*/s32[1]{0:T(128)}) custom-call(f32[2048,128]{1,0:T(8,128)} %x_hbm.1, s32[3,16]{1,0:T(4,128)} %partner_ref.1), custom_call_target="tpu_custom_call" | custom-call | tf_op jit(solution)/shard_map/start/pallas_call | solution.py:391
  21.6 63.2 %conditional.3 = ((f32[1024,128]{1,0:T(8,128)S(1)}, f32[1024,128]{1,0:T(8,128)S(1)}, f32[128,128]{1,0:T(8,128)S(1)})) conditional(s32[]{:T(128)} %bitcast.2, (f32[1024,128]{1,0:T(8,128)S(1)}, f32[1024,128]{1,0:T(8,128)S(1)}, f32[128,128]{1,0:T(8,128)S(1)}) %tuple.33, (f32[1024,128]{1,0:T(8,128)S(1)}, ...), branch_computations={%region_0.0_spmd, %region_1.0_spmd, %region_2.0_spmd, %region_3.0_... | conditional | bytes 8 | solution.py:393
  21.6 63.2 %turn3.3 = (f32[1024,128]{1,0:T(8,128)S(1)}, f32[1024,128]{1,0:T(8,128)S(1)}, f32[128,128]{1,0:T(8,128)S(1)}) custom-call(f32[1024,128]{1,0:T(8,128)S(1)} %get-tuple-element.86.p_ref, f32[1024,128]{1,0:T(8,128)S(1)} %get-tuple-element.87.q_ref, f32[128,128]{1,0:T(8,128)S(1)} %get-tuple-element.88.g_ref), custom_call_target="tpu_custom_call" | custom-call | tf_op jit(solution)/shard_map/cond/branch_3_fun/turn3/pallas_call | solution.py:393
  84.8 62.5 %conditional.4 = ((f32[1024,128]{1,0:T(8,128)S(1)}, f32[1024,128]{1,0:T(8,128)S(1)}, f32[128,128]{1,0:T(8,128)S(1)})) conditional(s32[]{:T(128)} %bitcast.1, (f32[1024,128]{1,0:T(8,128)S(1)}, f32[1024,128]{1,0:T(8,128)S(1)}, f32[128,128]{1,0:T(8,128)S(1)}) %get-tuple-element.167, (f32[1024,128]{1,0:T(8,128)S(1)}, ...), branch_computations={%region_4.0_spmd, %region_5.0_spmd, %region_6.0_spmd, %region_7.0_... | conditional | bytes 8 | solution.py:393
  85.0 62.3 %turn2.4 = (f32[1024,128]{1,0:T(8,128)S(1)}, f32[1024,128]{1,0:T(8,128)S(1)}, f32[128,128]{1,0:T(8,128)S(1)}) custom-call(f32[1024,128]{1,0:T(8,128)S(1)} %get-tuple-element.95.p_ref, f32[1024,128]{1,0:T(8,128)S(1)} %get-tuple-element.96.q_ref, f32[128,128]{1,0:T(8,128)S(1)} %get-tuple-element.97.g_ref), custom_call_target="tpu_custom_call" | custom-call | tf_op jit(solution)/shard_map/cond/branch_2_fun/turn2/pallas_call | solution.py:393
  147.3 32.7 %conditional.5 = ((f32[1024,128]{1,0:T(8,128)S(1)}, f32[1024,128]{1,0:T(8,128)S(1)}, f32[128,128]{1,0:T(8,128)S(1)})) conditional(s32[]{:T(128)} %bitcast, (f32[1024,128]{1,0:T(8,128)S(1)}, f32[1024,128]{1,0:T(8,128)S(1)}, f32[128,128]{1,0:T(8,128)S(1)}) %get-tuple-element.168, (f32[1024,128]{1,0:T(8,128)S(1)}, ...), branch_computations={%region_8.0_spmd, %region_9.0_spmd, %region_10.0_spmd, %region_11.... | conditional | bytes 8 | solution.py:393
  147.4 32.6 %turn1.5 = (f32[1024,128]{1,0:T(8,128)S(1)}, f32[1024,128]{1,0:T(8,128)S(1)}, f32[128,128]{1,0:T(8,128)S(1)}) custom-call(f32[1024,128]{1,0:T(8,128)S(1)} %get-tuple-element.104.p_ref, f32[1024,128]{1,0:T(8,128)S(1)} %get-tuple-element.105.q_ref, f32[128,128]{1,0:T(8,128)S(1)} %get-tuple-element.106.g_ref), custom_call_target="tpu_custom_call" | custom-call | tf_op jit(solution)/shard_map/cond/branch_1_fun/turn1/pallas_call | solution.py:393
  180.0 5.1 %last.1 = f32[2048,128]{1,0:T(8,128)} custom-call(f32[1024,128]{1,0:T(8,128)S(1)} %get-tuple-element.128.p_ref, f32[1024,128]{1,0:T(8,128)S(1)} %get-tuple-element.129.q_ref, f32[128,128]{1,0:T(8,128)S(1)} %get-tuple-element.130.g_ref), custom_call_target="tpu_custom_call" | custom-call | tf_op jit(solution)/shard_map/last/pallas_call | solution.py:394
